TPU v7x, 256 devices: a whole 4x4x8 slice. The times are simulated.
256 devices in a mesh: layer: 2 (over x_lo), row: 32 (over z, y), col: 4 (over x_hi, core).
Axes of the slice: x: 4 (x_hi: 2, x_lo: 2; x = x_hi * 2 + x_lo), y: 4, z: 8, core: 2. Of those that a mesh axis runs over, the one named last changes fastest.
Arguments:
- rhs_root: float32 [16384, 128], P('col'), may hold values from -6 to 6
- rhs_child: float32 [2, 8192, 128], P('layer', 'col'), may hold values from -6 to 6
- rhs_leaf: float32 [4, 4096, 128], P('layer', 'col'), may hold values from -6 to 6
- root_inv: bfloat16 [16384, 16384], P('row', 'col'), may hold values from -0.046875 to 0.046875
- child_inv: bfloat16 [2, 8192, 8192], P('layer', 'row', 'col'), may hold values from -0.0625 to 0.0625
- leaf_inv: bfloat16 [4, 4096, 4096], P('layer', 'row', 'col'), may hold values from -0.09375 to 0.09375
- leaf_to_child: bfloat16 [4, 8192, 4096], P('layer', 'col', 'row'), may hold values from -0.0625 to 0.0625
- leaf_to_root: bfloat16 [4, 16384, 4096], P('layer', 'col', 'row'), may hold values from -0.03125 to 0.03125
- child_to_root: bfloat16 [2, 16384, 8192], P('layer', 'col', 'row'), may hold values from -0.03125 to 0.03125
Outputs:
- x_root: float32 [16384, 128], P('col')
- x_child: float32 [2, 8192, 128], P('layer', 'col')
- x_leaf: float32 [4, 4096, 128], P('layer', 'col')
- y_root: float32 [16384, 128], P('row')
All inputs are finite; a program needn't handle non-finite values.
Results may differ from a plain program's by a relative error of at most 0.008.
Values sent between devices are 32-bit elements; how exact they have to be, the bound alone decides.
No kernel may reach another device: no remote copies, remote signals or barrier semaphores. Data moves between devices by JAX's collectives and lax.ppermute only.
A program may use at most 64 MiB of HBM per device.

v0:
```python
import jax
import jax.numpy as jnp
from jax import lax
from jax.sharding import PartitionSpec as P


def col_sum(values):
    return lax.psum(values, "col")


def row_sum(values):
    return lax.psum(values, "row")


def root_total(values):
    return lax.psum(values, ("layer", "row"))


def half16(values):
    return values.astype(jnp.bfloat16)


def on_device(
    rhs_root,
    rhs_child,
    rhs_leaf,
    root_inv,
    child_inv,
    leaf_inv,
    leaf_to_child,
    leaf_to_root,
    child_to_root,
):
    f32 = jnp.float32
    y_leaf = col_sum(
        jnp.einsum("gij,gjs->gis", leaf_inv, half16(rhs_leaf), preferred_element_type=f32)
    )
    leaf_bf = half16(y_leaf)
    leaf_update = jnp.einsum("gij,gjs->is", leaf_to_root, leaf_bf, preferred_element_type=f32)
    r_child = rhs_child[0] - row_sum(
        jnp.einsum("gij,gjs->is", leaf_to_child, leaf_bf, preferred_element_type=f32)
    )
    y_child = col_sum(jnp.dot(child_inv[0], half16(r_child), preferred_element_type=f32))
    child_update = jnp.dot(child_to_root[0], half16(y_child), preferred_element_type=f32)
    r_root = rhs_root - root_total(child_update + leaf_update)
    y_root = col_sum(jnp.dot(root_inv, half16(r_root), preferred_element_type=f32))
    x_root = row_sum(jnp.einsum("ij,is->js", root_inv, half16(y_root), preferred_element_type=f32))
    root_bf = half16(x_root)
    back_child = y_child - col_sum(
        jnp.einsum("ij,is->js", child_to_root[0], root_bf, preferred_element_type=f32)
    )
    x_child = row_sum(
        jnp.einsum("ij,is->js", child_inv[0], half16(back_child), preferred_element_type=f32)
    )
    terms = jnp.einsum("gij,is->gjs", leaf_to_child, half16(x_child), preferred_element_type=f32)
    terms = terms + jnp.einsum("gij,is->gjs", leaf_to_root, root_bf, preferred_element_type=f32)
    back_leaf = y_leaf - col_sum(terms)
    x_leaf = row_sum(
        jnp.einsum("gij,gis->gjs", leaf_inv, half16(back_leaf), preferred_element_type=f32)
    )
    return (x_root, x_child[None], x_leaf, y_root)


def solution(mesh):
    in_specs = (
        P("col", None),
        P("layer", "col", None),
        P("layer", "col", None),
        P("row", "col"),
        P("layer", "row", "col"),
        P("layer", "row", "col"),
        P("layer", "col", "row"),
        P("layer", "col", "row"),
        P("layer", "col", "row"),
    )
    out_specs = (P("col", None), P("layer", "col", None), P("layer", "col", None), P("row", None))
    return jax.shard_map(
        on_device, mesh=mesh, in_specs=in_specs, out_specs=out_specs, check_vma=False
    )
```

profile of v0, /device:TPU:2, one launch (start us, length us, event | category | flops | bytes accessed | tf_op | source)
XLA Modules:
  0.0 1495.1 jit_solution(6463682180785090896)
XLA Ops:
  7.2 0.0 copy-start
  7.2 0.0 all-reduce.11.cloned.1.call-start
  7.2 2.5 fusion.18
  9.7 0.0 all-reduce.11.cloned.1.call-update
  9.7 0.0 all-reduce.13.cloned.1.call-start
  9.8 48.8 %all-reduce.11.cloned.1.call-done = f32[2,128,128]{2,1,0:T(8,128)} async-done(((f32[2,128,128]{2,1,0:T(8,128)}), f32[2,128,128]{2,1,0:T(8,128)}) %all-reduce.11.cloned.1.call-update) | async-done | bytes 131088 | tf_op jit(solution)/shard_map/psum | solution.py:8
  58.5 2.6 convolution_bitcast_fusion.2
  61.2 0.0 all-reduce.13.cloned.1.call-update
  61.2 0.0 all-reduce.15.cloned.1.call-start
  61.2 152.3 %all-reduce.13.cloned.1.call-done = f32[2048,128]{1,0:T(8,128)} async-done(((f32[2048,128]{1,0:T(8,128)}), f32[2048,128]{1,0:T(8,128)}) %all-reduce.13.cloned.1.call-update) | async-done | bytes 1048592 | tf_op jit(solution)/shard_map/psum | solution.py:12
  213.5 2.7 convolution_bitcast_fusion.6
  216.2 0.0 all-reduce.15.cloned.1.call-update
  216.3 0.0 all-reduce.17.cloned.1.call-start
  216.3 3.6 convolution_bitcast_fusion
  219.9 38.4 %all-reduce.15.cloned.1.call-done = f32[256,128]{0,1:T(8,128)} async-done(((f32[256,128]{0,1:T(8,128)}), f32[256,128]{0,1:T(8,128)}) %all-reduce.15.cloned.1.call-update) | async-done | bytes 131088 | tf_op jit(solution)/shard_map/psum | solution.py:8
  258.3 3.7 fusion
  262.0 0.0 all-reduce.17.cloned.1.call-update
  262.0 0.0 all-reduce.19.cloned.1.call-start
  262.1 612.7 %all-reduce.17.cloned.1.call-done = f32[4096,128]{1,0:T(8,128)} async-done(((f32[4096,128]{1,0:T(8,128)}), f32[4096,128]{1,0:T(8,128)}) %all-reduce.17.cloned.1.call-update) | async-done | bytes 2097168 | tf_op jit(solution)/shard_map/psum | solution.py:16
  874.8 5.7 convolution_bitcast_fusion.5
  880.5 0.0 all-reduce.19.cloned.1.call-update
  880.6 0.0 all-reduce.21.cloned.1.call-start
  880.6 43.7 %all-reduce.19.cloned.1.call-done = f32[512,128]{0,1:T(8,128)} async-done(((f32[512,128]{0,1:T(8,128)}), f32[512,128]{0,1:T(8,128)}) %all-reduce.19.cloned.1.call-update) | async-done | bytes 262160 | tf_op jit(solution)/shard_map/psum | solution.py:8
  924.4 4.3 convolution_bitcast_fusion.1
  928.7 0.0 all-reduce.21.cloned.1.call-update
  928.7 0.0 all-reduce.23.cloned.1.call-start
  928.8 154.9 %all-reduce.21.cloned.1.call-done = f32[4096,128]{0,1:T(8,128)} async-done(((f32[4096,128]{0,1:T(8,128)}), f32[4096,128]{0,1:T(8,128)}) %all-reduce.21.cloned.1.call-update) | async-done | bytes 2097168 | tf_op jit(solution)/shard_map/psum | solution.py:12
  1083.7 2.7 fusion.4
  1086.4 0.0 all-reduce.23.cloned.1.call-update
  1086.4 0.0 all-reduce.25.cloned.1.call-start
  1086.5 42.2 %all-reduce.23.cloned.1.call-done = f32[256,128]{0,1:T(8,128)} async-done(((f32[256,128]{0,1:T(8,128)}), f32[256,128]{0,1:T(8,128)}) %all-reduce.23.cloned.1.call-update) | async-done | bytes 131088 | tf_op jit(solution)/shard_map/psum | solution.py:8
  1128.7 2.2 convolution_bitcast_fusion.3
  1130.9 0.0 all-reduce.25.cloned.1.call-update
  1130.9 0.0 all-reduce.27.cloned.1.call-start
  1131.0 152.7 %all-reduce.25.cloned.1.call-done = f32[2048,128]{0,1:T(8,128)} async-done(((f32[2048,128]{0,1:T(8,128)}), f32[2048,128]{0,1:T(8,128)}) %all-reduce.25.cloned.1.call-update) | async-done | bytes 1048592 | tf_op jit(solution)/shard_map/psum | solution.py:12
  1283.7 2.2 fusion.13
  1285.9 0.0 copy-start.4
  1285.9 3.1 fusion.7
  1289.1 0.0 all-reduce.27.cloned.1.call-update
  1289.1 0.0 all-reduce.29.cloned.1.call-start
  1289.2 41.6 %all-reduce.27.cloned.1.call-done = f32[2,128,128]{2,1,0:T(8,128)} async-done(((f32[2,128,128]{2,1,0:T(8,128)}), f32[2,128,128]{2,1,0:T(8,128)}) %all-reduce.27.cloned.1.call-update) | async-done | bytes 131088 | tf_op jit(solution)/shard_map/psum | solution.py:8
  1330.8 2.2 convolution_bitcast_fusion.4
  1333.0 0.0 all-reduce.29.cloned.1.call-update
  1333.1 0.8 copy.17
  1333.9 3.0 copy.14
  1336.9 1.3 copy.15
  1338.2 147.5 %all-reduce.29.cloned.1.call-done = f32[2,1024,128]{1,2,0:T(8,128)} async-done(((f32[2,1024,128]{1,2,0:T(8,128)}), f32[2,1024,128]{1,2,0:T(8,128)}) %all-reduce.29.cloned.1.call-update) | async-done | bytes 1048592 | tf_op jit(solution)/shard_map/psum | solution.py:12
  1485.7 2.5 copy.16
  (14 shorter events, 0.0 us)
Async XLA Ops:
  7.2 251.2 %copy-start = (bf16[1,4096,256]{2,1,0:T(8,128)(2,1)S(1)}, bf16[1,4096,256]{2,1,0:T(8,128)(2,1)}, u32[]{:S(2)}) copy-start(bf16[1,4096,256]{2,1,0:T(8,128)(2,1)} %param.17) | copy-start | bytes 6291460
  7.2 51.4 %all-reduce.11.cloned.1.call-start = ((), (), s32[]{:S(2)}) async-start(), calls=%async_computation | async-start | bytes 262144 | tf_op jit(solution)/shard_map/psum | solution.py:8
  9.7 203.8 %copy-start.2 = (bf16[1,256,2048]{2,1,0:T(8,128)(2,1)S(1)}, bf16[1,256,2048]{2,1,0:T(8,128)(2,1)}, u32[]{:S(2)}) copy-start(bf16[1,256,2048]{2,1,0:T(8,128)(2,1)} %param.13) | copy-start | bytes 3145732
  9.7 203.8 %all-reduce.13.cloned.1.call-start = ((), (), s32[]{:S(2)}) async-start(), calls=%async_computation.1 | async-start | bytes 2097152 | tf_op jit(solution)/shard_map/psum | solution.py:12
  61.2 155.1 %copy-start.5 = (f32[2,128,128]{2,1,0:T(8,128)S(1)}, f32[2,128,128]{2,1,0:T(8,128)}, u32[]{:S(2)}) copy-start(f32[2,128,128]{2,1,0:T(8,128)} %all-reduce.11.cloned.1.call-done) | copy-start | bytes 393220
  61.2 197.1 %all-reduce.15.cloned.1.call-start = ((), (), s32[]{:S(2)}) async-start(), calls=%async_computation.2 | async-start | bytes 262144 | tf_op jit(solution)/shard_map/psum | solution.py:8
  216.3 658.6 %all-reduce.17.cloned.1.call-start = ((), (), s32[]{:S(2)}) async-start(), calls=%async_computation.3 | async-start | bytes 4194304 | tf_op jit(solution)/shard_map/psum | solution.py:16
  262.0 662.3 %all-reduce.19.cloned.1.call-start = ((), (), s32[]{:S(2)}) async-start(), calls=%async_computation.4 | async-start | bytes 524288 | tf_op jit(solution)/shard_map/psum | solution.py:8
  880.6 203.1 %all-reduce.21.cloned.1.call-start = ((), (), s32[]{:S(2)}) async-start(), calls=%async_computation.5 | async-start | bytes 4194304 | tf_op jit(solution)/shard_map/psum | solution.py:12
  928.7 200.0 %copy-start.7 = (f32[256,128]{0,1:T(8,128)S(1)}, f32[256,128]{0,1:T(8,128)}, u32[]{:S(2)}) copy-start(f32[256,128]{0,1:T(8,128)} %all-reduce.15.cloned.1.call-done) | copy-start | bytes 393220
  928.7 200.0 %all-reduce.23.cloned.1.call-start = ((), (), s32[]{:S(2)}) async-start(), calls=%async_computation.6 | async-start | bytes 262144 | tf_op jit(solution)/shard_map/psum | solution.py:8
  1086.4 197.3 %all-reduce.25.cloned.1.call-start = ((), (), s32[]{:S(2)}) async-start(), calls=%async_computation.7 | async-start | bytes 2097152 | tf_op jit(solution)/shard_map/psum | solution.py:12
  1130.9 199.9 %all-reduce.27.cloned.1.call-start = ((), (), s32[]{:S(2)}) async-start(), calls=%async_computation.8 | async-start | bytes 262144 | tf_op jit(solution)/shard_map/psum | solution.py:8
  1283.7 2.2 copy-start.1
  1285.9 44.9 %copy-start.4 = (bf16[2,128,1024]{2,1,0:T(8,128)(2,1)S(1)}, bf16[2,128,1024]{2,1,0:T(8,128)(2,1)}, u32[]{:S(2)}) copy-start(bf16[2,128,1024]{2,1,0:T(8,128)(2,1)} %param.14) | copy-start | bytes 1572868
  1289.1 44.0 %copy-start.6 = (f32[512,128]{0,1:T(8,128)S(1)}, f32[512,128]{0,1:T(8,128)}, u32[]{:S(2)}) copy-start(f32[512,128]{0,1:T(8,128)} %all-reduce.19.cloned.1.call-done) | copy-start | bytes 786436
  1289.1 196.6 %all-reduce.29.cloned.1.call-start = ((), (), s32[]{:S(2)}) async-start(), calls=%async_computation.9 | async-start | bytes 2097152 | tf_op jit(solution)/shard_map/psum | solution.py:12
  1333.9 3.0 copy-start.3
Sparse Core Ops, SparseCore 0:
  11.2 47.3 all-reduce.10
  62.6 150.9 all-reduce.12
  216.7 41.5 all-reduce.14
  262.2 612.6 all-reduce.16
  880.7 43.6 all-reduce.18
  928.8 154.8 all-reduce.20
  1086.9 41.7 all-reduce.22
  1132.7 150.9 all-reduce.24
  1289.2 41.5 all-reduce.26
  1334.7 150.9 all-reduce.28
where the time goes:
time: 1500 us
  waiting for transfers between devices  1440 us (96%)
  matrix products  37.6 us (3%)
    psum x1, waiting for transfers between devices, root_total(): return lax.psum(values, ('layer', 'row'))  613 us
    psum x4, waiting for transfers between devices, row_sum(): return lax.psum(values, 'row')  607 us
    psum x5, waiting for transfers between devices, col_sum(): return lax.psum(values, 'col')  215 us
  transfers between devices with their start and end apart: 10, of which 10 were waited for; matrix products, arithmetic and copies ran while one was open for 1% of the time, Pallas kernels for 0%

commit v1 on v0

--- a/solution.py
+++ b/solution.py
@@ -13,7 +13,7 @@
 
 
 def root_total(values):
-    return lax.psum(values, ("layer", "row"))
+    return lax.psum(lax.psum(values, "layer"), "row")
 
 
 def half16(values):

time: 1500 us -> 1120 us (0.75)
  waiting for transfers between devices: 1440 us -> 1060 us
    psum x1 -> x2, waiting for transfers between devices: 613 us -> 234 us  [root_total(): return lax.psum(lax.psum(values, 'layer'), 'row')]
  transfers between devices with their start and end apart: 10 -> 11, of which waited for: 10 -> 11; matrix products, arithmetic and copies ran while one was open for 1% -> 1% of each run, Pallas kernels for 0% -> 0%
where the time goes in v1:
time: 1120 us; the launch traced here: 1110 us
  waiting for transfers between devices  1060 us (95%)
  matrix products  37.6 us (3%)
  between operations  13.9 us (1%)
    psum x4, waiting for transfers between devices, row_sum(): return lax.psum(values, 'row')  608 us
    psum x2, waiting for transfers between devices, root_total(): return lax.psum(lax.psum(values, 'layer'), 'row')  234 us
    psum x5, waiting for transfers between devices, col_sum(): return lax.psum(values, 'col')  214 us
  transfers between devices with their start and end apart: 11, of which 11 were waited for; matrix products, arithmetic and copies ran while one was open for 1% of the time, Pallas kernels for 0%

profile of v1, /device:TPU:2, one launch (start us, length us, event | category | flops | bytes accessed | tf_op | source)
XLA Modules:
  0.0 1115.0 jit_solution(5426813346997227982)
XLA Ops:
  7.2 0.0 all-reduce.12.cloned.1.call-start
  7.2 2.5 fusion.18
  9.7 0.0 all-reduce.12.cloned.1.call-update
  9.7 0.0 all-reduce.14.cloned.1.call-start
  9.8 48.8 %all-reduce.12.cloned.1.call-done = f32[2,128,128]{2,1,0:T(8,128)} async-done(((f32[2,128,128]{2,1,0:T(8,128)}), f32[2,128,128]{2,1,0:T(8,128)}) %all-reduce.12.cloned.1.call-update) | async-done | bytes 131088 | tf_op jit(solution)/shard_map/psum | solution.py:8
  58.5 2.6 convolution_bitcast_fusion.2
  61.2 0.0 all-reduce.14.cloned.1.call-update
  61.2 0.0 all-reduce.16.cloned.1.call-start
  61.2 152.3 %all-reduce.14.cloned.1.call-done = f32[2048,128]{1,0:T(8,128)} async-done(((f32[2048,128]{1,0:T(8,128)}), f32[2048,128]{1,0:T(8,128)}) %all-reduce.14.cloned.1.call-update) | async-done | bytes 1048592 | tf_op jit(solution)/shard_map/psum | solution.py:12
  213.5 2.7 convolution_bitcast_fusion.6
  216.2 0.0 all-reduce.16.cloned.1.call-update
  216.3 0.0 all-reduce.18.cloned.1.call-start
  216.3 3.6 convolution_bitcast_fusion
  219.9 38.4 %all-reduce.16.cloned.1.call-done = f32[256,128]{0,1:T(8,128)} async-done(((f32[256,128]{0,1:T(8,128)}), f32[256,128]{0,1:T(8,128)}) %all-reduce.16.cloned.1.call-update) | async-done | bytes 131088 | tf_op jit(solution)/shard_map/psum | solution.py:8
  258.3 3.7 fusion
  262.0 0.0 all-reduce.18.cloned.1.call-update
  262.0 0.0 all-reduce.20.cloned.1.call-start
  262.1 74.1 %all-reduce.18.cloned.1.call-done = f32[4096,128]{1,0:T(8,128)} async-done(((f32[4096,128]{1,0:T(8,128)}), f32[4096,128]{1,0:T(8,128)}) %all-reduce.18.cloned.1.call-update) | async-done | bytes 2097168 | tf_op jit(solution)/shard_map/psum | solution.py:16
  336.2 0.0 all-reduce.22.cloned.1.call-start
  336.2 159.9 %all-reduce.20.cloned.1.call-done = f32[4096,128]{1,0:T(8,128)} async-done(((f32[4096,128]{1,0:T(8,128)}), f32[4096,128]{1,0:T(8,128)}) %all-reduce.20.cloned.1.call-update) | async-done | bytes 2097168 | tf_op jit(solution)/shard_map/psum | solution.py:16
  496.1 5.7 convolution_bitcast_fusion.5
  501.8 0.0 all-reduce.22.cloned.1.call-update
  501.8 0.0 all-reduce.24.cloned.1.call-start
  501.9 42.6 %all-reduce.22.cloned.1.call-done = f32[512,128]{0,1:T(8,128)} async-done(((f32[512,128]{0,1:T(8,128)}), f32[512,128]{0,1:T(8,128)}) %all-reduce.22.cloned.1.call-update) | async-done | bytes 262160 | tf_op jit(solution)/shard_map/psum | solution.py:8
  544.4 4.3 convolution_bitcast_fusion.1
  548.8 0.0 all-reduce.24.cloned.1.call-update
  548.8 0.0 all-reduce.26.cloned.1.call-start
  548.8 154.9 %all-reduce.24.cloned.1.call-done = f32[4096,128]{0,1:T(8,128)} async-done(((f32[4096,128]{0,1:T(8,128)}), f32[4096,128]{0,1:T(8,128)}) %all-reduce.24.cloned.1.call-update) | async-done | bytes 2097168 | tf_op jit(solution)/shard_map/psum | solution.py:12
  703.7 2.7 fusion.4
  706.4 0.0 all-reduce.26.cloned.1.call-update
  706.5 0.0 all-reduce.28.cloned.1.call-start
  706.5 42.2 %all-reduce.26.cloned.1.call-done = f32[256,128]{0,1:T(8,128)} async-done(((f32[256,128]{0,1:T(8,128)}), f32[256,128]{0,1:T(8,128)}) %all-reduce.26.cloned.1.call-update) | async-done | bytes 131088 | tf_op jit(solution)/shard_map/psum | solution.py:8
  748.8 2.2 convolution_bitcast_fusion.3
  750.9 0.0 all-reduce.28.cloned.1.call-update
  751.0 0.0 all-reduce.30.cloned.1.call-start
  751.0 152.7 %all-reduce.28.cloned.1.call-done = f32[2048,128]{0,1:T(8,128)} async-done(((f32[2048,128]{0,1:T(8,128)}), f32[2048,128]{0,1:T(8,128)}) %all-reduce.28.cloned.1.call-update) | async-done | bytes 1048592 | tf_op jit(solution)/shard_map/psum | solution.py:12
  903.8 2.2 fusion.13
  906.0 3.1 fusion.7
  909.2 0.0 all-reduce.30.cloned.1.call-update
  909.2 0.0 all-reduce.32.cloned.1.call-start
  909.2 41.6 %all-reduce.30.cloned.1.call-done = f32[2,128,128]{2,1,0:T(8,128)} async-done(((f32[2,128,128]{2,1,0:T(8,128)}), f32[2,128,128]{2,1,0:T(8,128)}) %all-reduce.30.cloned.1.call-update) | async-done | bytes 131088 | tf_op jit(solution)/shard_map/psum | solution.py:8
  950.9 2.2 convolution_bitcast_fusion.4
  953.1 0.0 all-reduce.32.cloned.1.call-update
  953.1 0.8 copy.17
  954.0 3.0 copy.14
  956.9 1.3 copy.15
  958.2 147.7 %all-reduce.32.cloned.1.call-done = f32[2,1024,128]{1,2,0:T(8,128)} async-done(((f32[2,1024,128]{1,2,0:T(8,128)}), f32[2,1024,128]{1,2,0:T(8,128)}) %all-reduce.32.cloned.1.call-update) | async-done | bytes 1048592 | tf_op jit(solution)/shard_map/psum | solution.py:12
  1105.9 2.5 copy.16
  (17 shorter events, 0.1 us)
Async XLA Ops:
  7.2 251.2 %copy-start = (bf16[1,4096,256]{2,1,0:T(8,128)(2,1)S(1)}, bf16[1,4096,256]{2,1,0:T(8,128)(2,1)}, u32[]{:S(2)}) copy-start(bf16[1,4096,256]{2,1,0:T(8,128)(2,1)} %param.17) | copy-start | bytes 6291460
  7.2 51.4 %all-reduce.12.cloned.1.call-start = ((), (), s32[]{:S(2)}) async-start(), calls=%async_computation | async-start | bytes 262144 | tf_op jit(solution)/shard_map/psum | solution.py:8
  9.7 203.8 %copy-start.2 = (bf16[1,256,2048]{2,1,0:T(8,128)(2,1)S(1)}, bf16[1,256,2048]{2,1,0:T(8,128)(2,1)}, u32[]{:S(2)}) copy-start(bf16[1,256,2048]{2,1,0:T(8,128)(2,1)} %param.13) | copy-start | bytes 3145732
  9.7 203.8 %all-reduce.14.cloned.1.call-start = ((), (), s32[]{:S(2)}) async-start(), calls=%async_computation.1 | async-start | bytes 2097152 | tf_op jit(solution)/shard_map/psum | solution.py:12
  61.2 155.1 %copy-start.5 = (f32[2,128,128]{2,1,0:T(8,128)S(1)}, f32[2,128,128]{2,1,0:T(8,128)}, u32[]{:S(2)}) copy-start(f32[2,128,128]{2,1,0:T(8,128)} %all-reduce.12.cloned.1.call-done) | copy-start | bytes 393220
  61.2 197.1 %all-reduce.16.cloned.1.call-start = ((), (), s32[]{:S(2)}) async-start(), calls=%async_computation.2 | async-start | bytes 262144 | tf_op jit(solution)/shard_map/psum | solution.py:8
  216.3 119.9 %all-reduce.18.cloned.1.call-start = ((), (), s32[]{:S(2)}) async-start(), calls=%async_computation.3 | async-start | bytes 4194304 | tf_op jit(solution)/shard_map/psum | solution.py:16
  262.0 234.1 %all-reduce.20.cloned.1.call-start = ((), (), s32[]{:S(2)}) async-start(), calls=%async_computation.4 | async-start | bytes 4194304 | tf_op jit(solution)/shard_map/psum | solution.py:16
  336.2 208.3 %all-reduce.22.cloned.1.call-start = ((), (), s32[]{:S(2)}) async-start(), calls=%async_computation.5 | async-start | bytes 524288 | tf_op jit(solution)/shard_map/psum | solution.py:8
  501.8 201.9 %all-reduce.24.cloned.1.call-start = ((), (), s32[]{:S(2)}) async-start(), calls=%async_computation.6 | async-start | bytes 4194304 | tf_op jit(solution)/shard_map/psum | solution.py:12
  548.8 200.0 %copy-start.7 = (f32[256,128]{0,1:T(8,128)S(1)}, f32[256,128]{0,1:T(8,128)}, u32[]{:S(2)}) copy-start(f32[256,128]{0,1:T(8,128)} %all-reduce.16.cloned.1.call-done) | copy-start | bytes 393220
  548.8 200.0 %all-reduce.26.cloned.1.call-start = ((), (), s32[]{:S(2)}) async-start(), calls=%async_computation.7 | async-start | bytes 262144 | tf_op jit(solution)/shard_map/psum | solution.py:8
  706.5 197.3 %all-reduce.28.cloned.1.call-start = ((), (), s32[]{:S(2)}) async-start(), calls=%async_computation.8 | async-start | bytes 2097152 | tf_op jit(solution)/shard_map/psum | solution.py:12
  751.0 199.9 %all-reduce.30.cloned.1.call-start = ((), (), s32[]{:S(2)}) async-start(), calls=%async_computation.9 | async-start | bytes 262144 | tf_op jit(solution)/shard_map/psum | solution.py:8
  903.8 2.2 copy-start.1
  906.0 44.9 %copy-start.4 = (bf16[2,128,1024]{2,1,0:T(8,128)(2,1)S(1)}, bf16[2,128,1024]{2,1,0:T(8,128)(2,1)}, u32[]{:S(2)}) copy-start(bf16[2,128,1024]{2,1,0:T(8,128)(2,1)} %param.14) | copy-start | bytes 1572868
  909.1 44.0 %copy-start.6 = (f32[512,128]{0,1:T(8,128)S(1)}, f32[512,128]{0,1:T(8,128)}, u32[]{:S(2)}) copy-start(f32[512,128]{0,1:T(8,128)} %all-reduce.22.cloned.1.call-done) | copy-start | bytes 786436
  909.2 196.8 %all-reduce.32.cloned.1.call-start = ((), (), s32[]{:S(2)}) async-start(), calls=%async_computation.10 | async-start | bytes 2097152 | tf_op jit(solution)/shard_map/psum | solution.py:12
  954.0 3.0 copy-start.3
Sparse Core Ops, SparseCore 0:
  11.2 47.3 all-reduce.11
  62.6 150.9 all-reduce.13
  216.7 41.5 all-reduce.15
  262.2 73.9 all-reduce.17
  339.5 156.5 all-reduce.19
  501.9 42.4 all-reduce.21
  548.9 154.8 all-reduce.23
  706.9 41.7 all-reduce.25
  752.8 150.9 all-reduce.27
  909.3 41.5 all-reduce.29
  954.9 150.9 all-reduce.31
